TPU v7x, 128 devices: a whole 4x4x4 slice. The times are simulated.
128 devices in a mesh: row: 8 (over y, core), col: 16 (over x, z).
Axes of the slice: x: 4, y: 4, z: 4, core: 2. Of those that a mesh axis runs over, the one named last changes fastest.
Arguments:
- b_tensor: bfloat16 [128, 1024, 1024], P('col', 'row'), may hold values from -6 to 6
- occ_green: bfloat16 [1024, 1024], P(('row', 'col')), may hold values from -0.1875 to 0.1875
- virt_green: bfloat16 [1024, 1024], P(('row', 'col')), may hold values from -0.1875 to 0.1875
- b_mask: int32 [1, 8, 8], replicated, may hold values 0 or 1
- occ_mask: int32 [8, 8], replicated, may hold values 0 or 1
- virt_mask: int32 [8, 8], replicated, may hold values 0 or 1
Outputs:
- chi: float32 [128, 128], P(('row', 'col'))
All inputs are finite; a program needn't handle non-finite values.
Results may differ from a plain program's by a relative error of at most 0.0041.
Values may be sent and summed in bfloat16 or wider, within the bound.
A program may use at most 64 MiB of HBM per device.

v0:
```python
import jax
import jax.numpy as jnp
from jax import lax
from jax.sharding import PartitionSpec as P

TILE = 128


def expand_pair(mask):
    return jnp.repeat(jnp.repeat(mask, TILE, axis=0), TILE, axis=1).astype(jnp.bfloat16)


def per_device(b_tensor, occ_green, virt_green, b_mask, occ_mask, virt_mask):
    col_index = lax.axis_index("col")
    row_index = lax.axis_index("row")
    p_count, m_count, n_basis = b_tensor.shape
    p_tiles = (col_index * p_count + jnp.arange(p_count, dtype=jnp.int32)) // TILE
    m_tiles = (row_index * m_count + jnp.arange(m_count, dtype=jnp.int32)) // TILE
    local_mask = jnp.take(jnp.take(b_mask, p_tiles, axis=0), m_tiles, axis=1).astype(jnp.bfloat16)
    masked = b_tensor * jnp.repeat(local_mask, TILE, axis=2)
    exchanged_b = lax.all_to_all(masked, "col", split_axis=2, concat_axis=0, tiled=True)
    virt_full = lax.all_gather(virt_green, ("row", "col"), axis=0, tiled=True) * expand_pair(
        virt_mask
    )
    occ_rows = lax.all_gather(occ_green, "col", axis=0, tiled=True)
    occ_rows = occ_rows * lax.dynamic_slice_in_dim(
        expand_pair(occ_mask), row_index * m_count, m_count, 0
    )
    inner = jnp.dot(masked.reshape(-1, n_basis), virt_full, preferred_element_type=jnp.float32)
    inner = inner.astype(jnp.bfloat16).reshape(masked.shape)
    outer = jnp.einsum(
        "lm,pms->pls",
        occ_rows,
        lax.all_gather(inner, "row", axis=1, tiled=True),
        preferred_element_type=jnp.float32,
    ).astype(jnp.bfloat16)
    moved = lax.all_to_all(outer, "col", split_axis=2, concat_axis=0, tiled=True)
    b_flat = exchanged_b.reshape(exchanged_b.shape[0], -1)
    y_flat = moved.reshape(moved.shape[0], -1)
    summed = lax.psum_scatter(
        lax.dot_general(
            y_flat, b_flat, (((1,), (1,)), ((), ())), preferred_element_type=jnp.float32
        ),
        ("row", "col"),
        scatter_dimension=0,
        tiled=True,
    )
    return summed * (-2.0 / n_basis)


def solution(mesh):
    return jax.shard_map(
        per_device,
        mesh=mesh,
        in_specs=(
            P("col", "row", None),
            P(("row", "col"), None),
            P(("row", "col"), None),
            P(),
            P(),
            P(),
        ),
        out_specs=P(("row", "col"), None),
        check_vma=False,
    )
```

profile of v0, /device:TPU:1, one launch (start us, length us, event | category | flops | bytes accessed | tf_op | source)
XLA Modules:
  0.0 387.0 jit_solution(18253904898014795396)
XLA Ops:
  6.5 0.0 all-gather.3.cloned.1.call-start
  6.5 0.7 all-gather.3.cloned.1.call-update
  7.3 0.0 all-gather.5.cloned.1.call-start
  7.4 0.8 broadcast_select_fusion
  8.1 0.8 gather_fusion
  8.9 0.2 fusion.3
  9.2 1.4 broadcast_in_dim.39
  10.5 0.0 copy-start.1
  10.5 2.3 reshape.157
  12.8 0.0 copy-done.1
  12.8 3.2 mul.24
  16.1 63.1 %all-gather.3.cloned.1.call-done = bf16[1024,1024]{1,0:T(8,128)(2,1)} async-done(((bf16[8,1024]{1,0:T(8,128)(2,1)}), bf16[1024,1024]{1,0:T(8,128)(2,1)}) %all-gather.3.cloned.1.call-update) | async-done | bytes 2097168 | tf_op jit(solution)/shard_map/all_gather | solution.py:22
  79.2 0.0 copy-start.3
  79.3 2.9 broadcast_in_dim.41
  82.2 0.0 copy-done.3
  82.2 3.7 fusion.2
  85.9 3.9 %copy.19 = bf16[8,128,1024]{1,2,0:T(8,128)(2,1)} copy(bf16[8,128,1024]{2,1,0:T(8,128)(2,1)} %bitcast.45) | data formatting | bytes 4194304 | tf_op jit(solution)/shard_map/reshape | solution.py:30
  89.8 0.0 all-gather.5.cloned.1.call-update
  89.9 2.9 copy.22
  92.8 0.0 copy-start.2
  92.8 4.2 %all-to-all-start.1 = ((bf16[8,128,1024]{1,0,2:T(8,128)(2,1)}), bf16[8,128,1024]{1,0,2:T(8,128)(2,1)S(1)}, u32[]{:S(2)}, u32[]{:S(2)}) async-start(bf16[8,128,1024]{1,0,2:T(8,128)(2,1)} %copy.22), calls=%async_computation.1 | async-start | bytes 4194304 | tf_op jit(solution)/shard_map/all_to_all | solution.py:21
  97.0 0.0 copy-done.2
  97.1 2.9 broadcast_in_dim.43
  100.0 0.0 copy-start
  100.1 2.0 copy.35
  102.0 0.0 copy-done
  102.0 36.4 %all_gather.11 = bf16[128,1024]{1,0:T(8,128)(2,1)S(1)} all-gather(bf16[8,1024]{1,0:T(8,128)(2,1)S(1)} %copy-done), channel_id=1, replica_groups=mesh['row'=8,'col'=16] {'col'}, dimensions={0}, use_global_device_ids=true | all-gather | bytes 278528 | tf_op jit(solution)/shard_map/all_gather | solution.py:25
  138.5 39.3 %all-gather.5.cloned.1.call-done = bf16[8,1024,1024]{1,2,0:T(8,128)(2,1)} async-done(((bf16[8,128,1024]{1,2,0:T(8,128)(2,1)}), bf16[8,1024,1024]{1,2,0:T(8,128)(2,1)}) %all-gather.5.cloned.1.call-update) | async-done | bytes 16777232 | tf_op jit(solution)/shard_map/all_gather | solution.py:34
  177.7 10.3 %convert_bitcast_fusion = bf16[8,128,1024]{1,2,0:T(8,128)(2,1)S(1)} fusion(bf16[8,1024,1024]{1,2,0:T(8,128)(2,1)} %all-gather.5.cloned.1.call-done, bf16[128,1024]{1,0:T(8,128)(2,1)S(1)} %all_gather.11, bf16[1024,1024]{1,0:T(8,128)(2,1)} %bitcast.44, s32[]{:T(128)S(6)} %select_n.83), kind=kOutput, calls=%fused_computation.5 | convolution fusion | flops 2149056512 | bytes 19398660 | tf_op jit(solution)/shard_map/lm,pms->pls/dot_general | solution.py:31
  188.0 2.7 copy.20
  190.7 0.0 all-to-all-done.1
  190.7 6.7 %all-to-all-start = ((bf16[8,128,1024]{1,0,2:T(8,128)(2,1)}), bf16[8,128,1024]{1,0,2:T(8,128)(2,1)}, u32[]{:S(2)}, u32[]{:S(2)}) async-start(bf16[8,128,1024]{1,0,2:T(8,128)(2,1)} %copy.20), calls=%async_computation | async-start | bytes 4194304 | tf_op jit(solution)/shard_map/all_to_all | solution.py:37
  197.5 0.0 all-reduce.3.cloned.1.call-start
  197.5 3.2 copy.24
  200.7 5.7 %reshape.161 = bf16[128,8192]{1,0:T(8,128)(2,1)S(1)} reshape(bf16[16,8,128,64]{3,2,1,0:T(8,128)(2,1)} %copy.24) | data formatting | bytes 4194304 | tf_op jit(solution)/shard_map/reshape | solution.py:38
  206.4 20.3 %all-to-all-done = bf16[8,128,1024]{1,0,2:T(8,128)(2,1)} async-done(((bf16[8,128,1024]{1,0,2:T(8,128)(2,1)}), bf16[8,128,1024]{1,0,2:T(8,128)(2,1)}, u32[]{:S(2)}, u32[]{:S(2)}) %all-to-all-start) | async-done | bytes 2097184 | tf_op jit(solution)/shard_map/all_to_all | solution.py:37
  226.7 4.8 %copy.21 = bf16[8,128,16,64]{3,1,0,2:T(8,128)(2,1)} copy(bf16[8,128,16,64]{1,0,3,2:T(8,128)(2,1)} %bitcast.9) | data formatting | bytes 4194304 | tf_op jit(solution)/shard_map/all_to_all | solution.py:37
  231.5 6.6 %reshape.160 = bf16[128,8192]{1,0:T(8,128)(2,1)} reshape(bf16[16,8,128,64]{3,2,1,0:T(8,128)(2,1)} %bitcast.39) | data formatting | bytes 4194304 | tf_op jit(solution)/shard_map/reshape | solution.py:39
  238.1 2.9 fusion.9
  241.1 0.0 all-reduce.3.cloned.1.call-update
  241.1 138.1 %all-reduce.3.cloned.1.call-done = f32[128,128]{1,0:T(8,128)} async-done(((f32[128,128]{1,0:T(8,128)}), f32[128,128]{1,0:T(8,128)}) %all-reduce.3.cloned.1.call-update) | async-done | bytes 65552
  379.2 1.2 dynamic-slice_multiply_fusion
  (9 shorter events, 0.2 us)
Async XLA Ops:
  6.5 72.7 %all-gather.3.cloned.1.call-start = ((), (), s32[]{:S(2)}) async-start(), calls=%async_computation.2 | async-start | bytes 2113536 | tf_op jit(solution)/shard_map/all_gather | solution.py:22
  7.3 170.5 %all-gather.5.cloned.1.call-start = ((), (), s32[]{:S(2)}) async-start(), calls=%async_computation.3 | async-start | bytes 18874368 | tf_op jit(solution)/shard_map/all_gather | solution.py:34
  10.5 2.3 copy-start.1
  79.2 3.0 copy-start.3
  92.8 4.2 %copy-start.2 = (s32[8,8]{1,0:T(8,128)S(1)}, s32[8,8]{1,0:T(8,128)}, u32[]{:S(2)}) copy-start(s32[8,8]{1,0:T(8,128)} %param.10) | copy-start | bytes 772
  92.8 97.9 %all-to-all-start.1 = ((bf16[8,128,1024]{1,0,2:T(8,128)(2,1)}), bf16[8,128,1024]{1,0,2:T(8,128)(2,1)S(1)}, u32[]{:S(2)}, u32[]{:S(2)}) async-start(bf16[8,128,1024]{1,0,2:T(8,128)(2,1)} %copy.22), calls=%async_computation.1 | async-start | bytes 4194304 | tf_op jit(solution)/shard_map/all_to_all | solution.py:21
  100.0 2.0 copy-start
  190.7 36.0 %all-to-all-start = ((bf16[8,128,1024]{1,0,2:T(8,128)(2,1)}), bf16[8,128,1024]{1,0,2:T(8,128)(2,1)}, u32[]{:S(2)}, u32[]{:S(2)}) async-start(bf16[8,128,1024]{1,0,2:T(8,128)(2,1)} %copy.20), calls=%async_computation | async-start | bytes 4194304 | tf_op jit(solution)/shard_map/all_to_all | solution.py:37
  197.5 181.8 %all-reduce.3.cloned.1.call-start = ((), (), s32[]{:S(2)}) async-start(), calls=%async_computation.4 | async-start | bytes 131072
Sparse Core Ops, SparseCore 0:
  10.3 68.8 all-gather.2
  90.0 87.6 all-gather.4
  241.2 137.9 all-reduce.2
where the time goes:
time: 388 us; the launch traced here: 387 us
  waiting for transfers between devices  262 us (68%)
  local copies, waits for them, and re-layouts  42.2 us (11%)
  blocking collectives  36.4 us (9%)
  matrix products  16.9 us (4%)
  between operations  13.3 us (3%)
  starting transfers between devices  11 us (3%)
  other arithmetic  5.47 us (1%)
    unnamed x4, waiting for transfers between devices  139 us
    all_gather x1, waiting for transfers between devices, per_device(): lax.all_gather(virt_green, ('row', 'col'), axis=0, tiled=True)  63.1 us
    all_gather x1, waiting for transfers between devices, per_device(): lax.all_gather(inner, 'row', axis=1, tiled=True)  39.3 us
    all_gather x1, blocking collectives, per_device(): occ_rows = lax.all_gather(occ_green, 'col', axis=0, tiled=True)  36.4 us
    all_to_all x1, waiting for transfers between devices, per_device(): lax.all_to_all(outer, 'col', split_axis=2, concat_axis=0, tiled=True)  20.3 us
    dot_general x1, matrix products, per_device(): jnp.einsum('lm,pms->pls', occ_rows, lax.all_gather(inner, 'row', axis=1,...  10.3 us
  transfers between devices with their start and end apart: 5, of which 4 were waited for; matrix products, arithmetic and copies ran while one was open for 10% of the time, Pallas kernels for 0%

commit v1 on v0

--- a/solution.py
+++ b/solution.py
@@ -22,7 +22,12 @@
     virt_full = lax.all_gather(virt_green, ("row", "col"), axis=0, tiled=True) * expand_pair(
         virt_mask
     )
-    occ_rows = lax.all_gather(occ_green, "col", axis=0, tiled=True)
+    ring = [occ_green]
+    for hop in range(15):
+        ring.append(lax.ppermute(ring[-1], "col", [(dev, (dev + 1) % 16) for dev in range(16)]))
+    occ_rows = jnp.roll(
+        jnp.concatenate(ring[::-1], axis=0), (lax.axis_index("col") + 1) * ring[0].shape[0], axis=0
+    )
     occ_rows = occ_rows * lax.dynamic_slice_in_dim(
         expand_pair(occ_mask), row_index * m_count, m_count, 0
     )

time: 388 us -> 403 us (1.039)
  waiting for transfers between devices: 262 us -> 311 us
  blocking collectives: 36.4 us -> 0 us
    ppermute x0 -> x15, waiting for transfers between devices: none -> 82.7 us  [per_device(): lax.ppermute(ring[-1], 'col', [(dev, (dev + 1) % 16) for dev in range(16)])]
    all_gather x1, waiting for transfers between devices: 39.3 us -> 0.02 us  [per_device(): lax.all_gather(inner, 'row', axis=1, tiled=True)]
    all_gather x1 -> x0, blocking collectives: 36.4 us -> none  [per_device(): occ_rows = lax.all_gather(occ_green, 'col', axis=0, tiled=True)]
    unnamed x4, waiting for transfers between devices: 139 us -> 153 us
    all_to_all x1, waiting for transfers between devices: 20.3 us -> 12.2 us  [per_device(): lax.all_to_all(outer, 'col', split_axis=2, concat_axis=0, tiled=True)]
  transfers between devices with their start and end apart: 5 -> 20, of which waited for: 4 -> 17; matrix products, arithmetic and copies ran while one was open for 10% -> 10% of each run, Pallas kernels for 0% -> 0%
where the time goes in v1:
time: 403 us
  waiting for transfers between devices  311 us (77%)
  local copies, waits for them, and re-layouts  43 us (11%)
  matrix products  16.9 us (4%)
  between operations  13.6 us (3%)
  starting transfers between devices  13.1 us (3%)
  other arithmetic  5.47 us (1%)
    unnamed x4, waiting for transfers between devices  153 us
    ppermute x15, waiting for transfers between devices, per_device(): lax.ppermute(ring[-1], 'col', [(dev, (dev + 1) % 16) for dev in range(16)])  82.7 us
    all_gather x1, waiting for transfers between devices, per_device(): lax.all_gather(virt_green, ('row', 'col'), axis=0, tiled=True)  63.1 us
    all_to_all x1, waiting for transfers between devices, per_device(): lax.all_to_all(outer, 'col', split_axis=2, concat_axis=0, tiled=True)  12.2 us
    dot_general x1, matrix products, per_device(): jnp.einsum('lm,pms->pls', occ_rows, lax.all_gather(inner, 'row', axis=1,...  10.3 us
  transfers between devices with their start and end apart: 20, of which 17 were waited for; matrix products, arithmetic and copies ran while one was open for 10% of the time, Pallas kernels for 0%

profile of v1, /device:TPU:1, one launch (start us, length us, event | category | flops | bytes accessed | tf_op | source)
XLA Modules:
  0.0 402.8 jit_solution(12785328611807869072)
XLA Ops:
  6.5 0.7 all-gather.3.cloned.1.call-update
  7.3 0.0 all-gather.5.cloned.1.call-start
  7.4 0.8 broadcast_select_fusion
  8.1 0.8 gather_fusion
  8.9 0.2 fusion.3
  9.2 1.4 broadcast_in_dim.39
  10.5 0.0 copy-start.1
  10.5 2.3 reshape.157
  12.8 3.2 mul.27
  16.1 63.1 %all-gather.3.cloned.1.call-done = bf16[1024,1024]{1,0:T(8,128)(2,1)} async-done(((bf16[8,1024]{1,0:T(8,128)(2,1)}), bf16[1024,1024]{1,0:T(8,128)(2,1)}) %all-gather.3.cloned.1.call-update) | async-done | bytes 2097168 | tf_op jit(solution)/shard_map/all_gather | solution.py:22
  79.3 2.9 broadcast_in_dim.41
  82.2 3.7 fusion.2
  85.9 3.9 copy.19
  89.8 0.0 all-gather.5.cloned.1.call-update
  89.9 0.7 copy-done
  90.6 0.0 collective-permute-start
  90.6 5.9 %collective-permute-done = bf16[8,1024]{1,0:T(8,128)(2,1)S(1)} collective-permute-done((bf16[8,1024]{1,0:T(8,128)(2,1)S(1)}, bf16[8,1024]{1,0:T(8,128)(2,1)S(1)}, u32[]{:S(2)}, u32[]{:S(2)}) %collective-permute-start) | collective-permute-done | bytes 16416 | tf_op jit(solution)/shard_map/ppermute | solution.py:27
  96.5 0.0 collective-permute-start.1
  96.5 5.9 %collective-permute-done.1 = bf16[8,1024]{1,0:T(8,128)(2,1)S(1)} collective-permute-done((bf16[8,1024]{1,0:T(8,128)(2,1)S(1)}, bf16[8,1024]{1,0:T(8,128)(2,1)S(1)}, u32[]{:S(2)}, u32[]{:S(2)}) %collective-permute-start.1) | collective-permute-done | bytes 16416 | tf_op jit(solution)/shard_map/ppermute | solution.py:27
  102.4 0.0 collective-permute-start.2
  102.4 5.9 %collective-permute-done.2 = bf16[8,1024]{1,0:T(8,128)(2,1)S(1)} collective-permute-done((bf16[8,1024]{1,0:T(8,128)(2,1)S(1)}, bf16[8,1024]{1,0:T(8,128)(2,1)S(1)}, u32[]{:S(2)}, u32[]{:S(2)}) %collective-permute-start.2) | collective-permute-done | bytes 16416 | tf_op jit(solution)/shard_map/ppermute | solution.py:27
  108.3 0.0 collective-permute-start.3
  108.3 5.9 %collective-permute-done.3 = bf16[8,1024]{1,0:T(8,128)(2,1)S(1)} collective-permute-done((bf16[8,1024]{1,0:T(8,128)(2,1)S(1)}, bf16[8,1024]{1,0:T(8,128)(2,1)S(1)}, u32[]{:S(2)}, u32[]{:S(2)}) %collective-permute-start.3) | collective-permute-done | bytes 16416 | tf_op jit(solution)/shard_map/ppermute | solution.py:27
  114.2 0.0 collective-permute-start.4
  114.2 5.9 %collective-permute-done.4 = bf16[8,1024]{1,0:T(8,128)(2,1)S(1)} collective-permute-done((bf16[8,1024]{1,0:T(8,128)(2,1)S(1)}, bf16[8,1024]{1,0:T(8,128)(2,1)S(1)}, u32[]{:S(2)}, u32[]{:S(2)}) %collective-permute-start.4) | collective-permute-done | bytes 16416 | tf_op jit(solution)/shard_map/ppermute | solution.py:27
  120.1 0.0 collective-permute-start.5
  120.1 5.9 %collective-permute-done.5 = bf16[8,1024]{1,0:T(8,128)(2,1)S(1)} collective-permute-done((bf16[8,1024]{1,0:T(8,128)(2,1)S(1)}, bf16[8,1024]{1,0:T(8,128)(2,1)S(1)}, u32[]{:S(2)}, u32[]{:S(2)}) %collective-permute-start.5) | collective-permute-done | bytes 16416 | tf_op jit(solution)/shard_map/ppermute | solution.py:27
  126.0 0.0 collective-permute-start.6
  126.0 5.9 %collective-permute-done.6 = bf16[8,1024]{1,0:T(8,128)(2,1)S(1)} collective-permute-done((bf16[8,1024]{1,0:T(8,128)(2,1)S(1)}, bf16[8,1024]{1,0:T(8,128)(2,1)S(1)}, u32[]{:S(2)}, u32[]{:S(2)}) %collective-permute-start.6) | collective-permute-done | bytes 16416 | tf_op jit(solution)/shard_map/ppermute | solution.py:27
  131.9 0.0 collective-permute-start.7
  131.9 5.9 %collective-permute-done.7 = bf16[8,1024]{1,0:T(8,128)(2,1)S(1)} collective-permute-done((bf16[8,1024]{1,0:T(8,128)(2,1)S(1)}, bf16[8,1024]{1,0:T(8,128)(2,1)S(1)}, u32[]{:S(2)}, u32[]{:S(2)}) %collective-permute-start.7) | collective-permute-done | bytes 16416 | tf_op jit(solution)/shard_map/ppermute | solution.py:27
  137.8 0.0 collective-permute-start.8
  137.8 5.9 %collective-permute-done.8 = bf16[8,1024]{1,0:T(8,128)(2,1)S(1)} collective-permute-done((bf16[8,1024]{1,0:T(8,128)(2,1)S(1)}, bf16[8,1024]{1,0:T(8,128)(2,1)S(1)}, u32[]{:S(2)}, u32[]{:S(2)}) %collective-permute-start.8) | collective-permute-done | bytes 16416 | tf_op jit(solution)/shard_map/ppermute | solution.py:27
  143.8 0.0 collective-permute-start.9
  143.8 5.9 %collective-permute-done.9 = bf16[8,1024]{1,0:T(8,128)(2,1)S(1)} collective-permute-done((bf16[8,1024]{1,0:T(8,128)(2,1)S(1)}, bf16[8,1024]{1,0:T(8,128)(2,1)S(1)}, u32[]{:S(2)}, u32[]{:S(2)}) %collective-permute-start.9) | collective-permute-done | bytes 16416 | tf_op jit(solution)/shard_map/ppermute | solution.py:27
  149.7 0.0 collective-permute-start.10
  149.7 5.9 %collective-permute-done.10 = bf16[8,1024]{1,0:T(8,128)(2,1)S(1)} collective-permute-done((bf16[8,1024]{1,0:T(8,128)(2,1)S(1)}, bf16[8,1024]{1,0:T(8,128)(2,1)S(1)}, u32[]{:S(2)}, u32[]{:S(2)}) %collective-permute-start.10) | collective-permute-done | bytes 16416 | tf_op jit(solution)/shard_map/ppermute | solution.py:27
  155.6 0.0 collective-permute-start.11
  155.6 5.9 %collective-permute-done.11 = bf16[8,1024]{1,0:T(8,128)(2,1)S(1)} collective-permute-done((bf16[8,1024]{1,0:T(8,128)(2,1)S(1)}, bf16[8,1024]{1,0:T(8,128)(2,1)S(1)}, u32[]{:S(2)}, u32[]{:S(2)}) %collective-permute-start.11) | collective-permute-done | bytes 16416 | tf_op jit(solution)/shard_map/ppermute | solution.py:27
  161.5 0.0 collective-permute-start.12
  161.5 5.9 %collective-permute-done.12 = bf16[8,1024]{1,0:T(8,128)(2,1)S(1)} collective-permute-done((bf16[8,1024]{1,0:T(8,128)(2,1)S(1)}, bf16[8,1024]{1,0:T(8,128)(2,1)S(1)}, u32[]{:S(2)}, u32[]{:S(2)}) %collective-permute-start.12) | collective-permute-done | bytes 16416 | tf_op jit(solution)/shard_map/ppermute | solution.py:27
  167.4 0.0 collective-permute-start.13
  167.4 5.9 %collective-permute-done.13 = bf16[8,1024]{1,0:T(8,128)(2,1)S(1)} collective-permute-done((bf16[8,1024]{1,0:T(8,128)(2,1)S(1)}, bf16[8,1024]{1,0:T(8,128)(2,1)S(1)}, u32[]{:S(2)}, u32[]{:S(2)}) %collective-permute-start.13) | collective-permute-done | bytes 16416 | tf_op jit(solution)/shard_map/ppermute | solution.py:27
  173.3 0.0 collective-permute-start.14
  173.3 2.9 copy.22
  176.2 6.3 %all-to-all-start.1 = ((bf16[8,128,1024]{1,0,2:T(8,128)(2,1)}), bf16[8,128,1024]{1,0,2:T(8,128)(2,1)S(1)}, u32[]{:S(2)}, u32[]{:S(2)}) async-start(bf16[8,128,1024]{1,0,2:T(8,128)(2,1)} %copy.22), calls=%async_computation.1 | async-start | bytes 4194304 | tf_op jit(solution)/shard_map/all_to_all | solution.py:21
  182.6 2.9 broadcast_in_dim.43
  185.5 2.0 copy.35
  187.5 0.0 collective-permute-done.14
  187.9 0.0 all-gather.5.cloned.1.call-done
  187.9 10.3 %convert_bitcast_fusion = bf16[8,128,1024]{1,2,0:T(8,128)(2,1)S(1)} fusion(bf16[8,1024,1024]{1,2,0:T(8,128)(2,1)} %all-gather.5.cloned.1.call-done, bf16[1024,1024]{1,0:T(8,128)(2,1)} %bitcast.44, s32[]{:T(128)S(6)} %select_n.98, bf16[256,1024]{1,0:T(8,128)(2,1)S(1)} %constant_dynamic-update-slice_fusion, s32[]{:T(128)S(6)} %select_n.97), kind=kOutput, calls=%fused_computation.5 | convolution fusion | flops 2149056512 | bytes 19398664 | tf_op jit(solution)/shard_map/lm,pms->pls/dot_general | solution.py:36
  198.2 2.8 copy.20
  201.0 0.0 all-to-all-done.1
  201.0 6.7 %all-to-all-start = ((bf16[8,128,1024]{1,0,2:T(8,128)(2,1)}), bf16[8,128,1024]{1,0,2:T(8,128)(2,1)}, u32[]{:S(2)}, u32[]{:S(2)}) async-start(bf16[8,128,1024]{1,0,2:T(8,128)(2,1)} %copy.20), calls=%async_computation | async-start | bytes 4194304 | tf_op jit(solution)/shard_map/all_to_all | solution.py:42
  207.7 0.0 all-reduce.3.cloned.1.call-start
  207.7 3.2 copy.24
  210.9 5.7 %reshape.161 = bf16[128,8192]{1,0:T(8,128)(2,1)S(1)} reshape(bf16[16,8,128,64]{3,2,1,0:T(8,128)(2,1)} %copy.24) | data formatting | bytes 4194304 | tf_op jit(solution)/shard_map/reshape | solution.py:43
  216.6 12.2 %all-to-all-done = bf16[8,128,1024]{1,0,2:T(8,128)(2,1)} async-done(((bf16[8,128,1024]{1,0,2:T(8,128)(2,1)}), bf16[8,128,1024]{1,0,2:T(8,128)(2,1)}, u32[]{:S(2)}, u32[]{:S(2)}) %all-to-all-start) | async-done | bytes 2097184 | tf_op jit(solution)/shard_map/all_to_all | solution.py:42
  228.7 4.8 %copy.21 = bf16[8,128,16,64]{3,1,0,2:T(8,128)(2,1)} copy(bf16[8,128,16,64]{1,0,3,2:T(8,128)(2,1)} %bitcast.9) | data formatting | bytes 4194304 | tf_op jit(solution)/shard_map/all_to_all | solution.py:42
  233.5 6.6 %reshape.160 = bf16[128,8192]{1,0:T(8,128)(2,1)} reshape(bf16[16,8,128,64]{3,2,1,0:T(8,128)(2,1)} %bitcast.39) | data formatting | bytes 4194304 | tf_op jit(solution)/shard_map/reshape | solution.py:44
  240.1 2.9 fusion.10
  243.1 0.0 all-reduce.3.cloned.1.call-update
  243.1 152.0 %all-reduce.3.cloned.1.call-done = f32[128,128]{1,0:T(8,128)} async-done(((f32[128,128]{1,0:T(8,128)}), f32[128,128]{1,0:T(8,128)}) %all-reduce.3.cloned.1.call-update) | async-done | bytes 65552
  395.1 1.2 dynamic-slice_multiply_fusion
  (48 shorter events, 0.3 us)
Async XLA Ops:
  6.5 72.7 %all-gather.3.cloned.1.call-start = ((), (), s32[]{:S(2)}) async-start(), calls=%async_computation.2 | async-start | bytes 2113536 | tf_op jit(solution)/shard_map/all_gather | solution.py:22
  7.3 180.6 %all-gather.5.cloned.1.call-start = ((), (), s32[]{:S(2)}) async-start(), calls=%async_computation.3 | async-start | bytes 18874368 | tf_op jit(solution)/shard_map/all_gather | solution.py:39
  10.5 2.3 copy-start.1
  79.2 3.0 copy-start.3
  89.8 0.7 copy-start
  90.6 5.9 %collective-permute-start = (bf16[8,1024]{1,0:T(8,128)(2,1)S(1)}, bf16[8,1024]{1,0:T(8,128)(2,1)S(1)}, u32[]{:S(2)}, u32[]{:S(2)}) collective-permute-start(bf16[8,1024]{1,0:T(8,128)(2,1)S(1)} %copy-done), channel_id=1, source_target_pairs={{0,1},{1,2},{2,3},{3,4},{4,5},{5,6},{6,7},{7,8},{8,9},{9,10},{10,1... | collective-permute-start | bytes 49160 | tf_op jit(solution)/shard_map/ppermute | solution.py:27
  96.5 5.9 %collective-permute-start.1 = (bf16[8,1024]{1,0:T(8,128)(2,1)S(1)}, bf16[8,1024]{1,0:T(8,128)(2,1)S(1)}, u32[]{:S(2)}, u32[]{:S(2)}) collective-permute-start(bf16[8,1024]{1,0:T(8,128)(2,1)S(1)} %collective-permute-done), channel_id=1, source_target_pairs={{0,1},{1,2},{2,3},{3,4},{4,5},{5,6},{6,7},{7,8},{8,9},{9,10},{10,1... | collective-permute-start | bytes 49160 | tf_op jit(solution)/shard_map/ppermute | solution.py:27
  102.4 5.9 %collective-permute-start.2 = (bf16[8,1024]{1,0:T(8,128)(2,1)S(1)}, bf16[8,1024]{1,0:T(8,128)(2,1)S(1)}, u32[]{:S(2)}, u32[]{:S(2)}) collective-permute-start(bf16[8,1024]{1,0:T(8,128)(2,1)S(1)} %collective-permute-done.1), channel_id=1, source_target_pairs={{0,1},{1,2},{2,3},{3,4},{4,5},{5,6},{6,7},{7,8},{8,9},{9,10},{10,1... | collective-permute-start | bytes 49160 | tf_op jit(solution)/shard_map/ppermute | solution.py:27
  108.3 5.9 %collective-permute-start.3 = (bf16[8,1024]{1,0:T(8,128)(2,1)S(1)}, bf16[8,1024]{1,0:T(8,128)(2,1)S(1)}, u32[]{:S(2)}, u32[]{:S(2)}) collective-permute-start(bf16[8,1024]{1,0:T(8,128)(2,1)S(1)} %collective-permute-done.2), channel_id=1, source_target_pairs={{0,1},{1,2},{2,3},{3,4},{4,5},{5,6},{6,7},{7,8},{8,9},{9,10},{10,1... | collective-permute-start | bytes 49160 | tf_op jit(solution)/shard_map/ppermute | solution.py:27
  114.2 5.9 %collective-permute-start.4 = (bf16[8,1024]{1,0:T(8,128)(2,1)S(1)}, bf16[8,1024]{1,0:T(8,128)(2,1)S(1)}, u32[]{:S(2)}, u32[]{:S(2)}) collective-permute-start(bf16[8,1024]{1,0:T(8,128)(2,1)S(1)} %collective-permute-done.3), channel_id=1, source_target_pairs={{0,1},{1,2},{2,3},{3,4},{4,5},{5,6},{6,7},{7,8},{8,9},{9,10},{10,1... | collective-permute-start | bytes 49160 | tf_op jit(solution)/shard_map/ppermute | solution.py:27
  120.1 5.9 %collective-permute-start.5 = (bf16[8,1024]{1,0:T(8,128)(2,1)S(1)}, bf16[8,1024]{1,0:T(8,128)(2,1)S(1)}, u32[]{:S(2)}, u32[]{:S(2)}) collective-permute-start(bf16[8,1024]{1,0:T(8,128)(2,1)S(1)} %collective-permute-done.4), channel_id=1, source_target_pairs={{0,1},{1,2},{2,3},{3,4},{4,5},{5,6},{6,7},{7,8},{8,9},{9,10},{10,1... | collective-permute-start | bytes 49160 | tf_op jit(solution)/shard_map/ppermute | solution.py:27
  126.0 5.9 %collective-permute-start.6 = (bf16[8,1024]{1,0:T(8,128)(2,1)S(1)}, bf16[8,1024]{1,0:T(8,128)(2,1)S(1)}, u32[]{:S(2)}, u32[]{:S(2)}) collective-permute-start(bf16[8,1024]{1,0:T(8,128)(2,1)S(1)} %collective-permute-done.5), channel_id=1, source_target_pairs={{0,1},{1,2},{2,3},{3,4},{4,5},{5,6},{6,7},{7,8},{8,9},{9,10},{10,1... | collective-permute-start | bytes 49160 | tf_op jit(solution)/shard_map/ppermute | solution.py:27
  131.9 5.9 %collective-permute-start.7 = (bf16[8,1024]{1,0:T(8,128)(2,1)S(1)}, bf16[8,1024]{1,0:T(8,128)(2,1)S(1)}, u32[]{:S(2)}, u32[]{:S(2)}) collective-permute-start(bf16[8,1024]{1,0:T(8,128)(2,1)S(1)} %collective-permute-done.6), channel_id=1, source_target_pairs={{0,1},{1,2},{2,3},{3,4},{4,5},{5,6},{6,7},{7,8},{8,9},{9,10},{10,1... | collective-permute-start | bytes 49160 | tf_op jit(solution)/shard_map/ppermute | solution.py:27
  137.8 5.9 %collective-permute-start.8 = (bf16[8,1024]{1,0:T(8,128)(2,1)S(1)}, bf16[8,1024]{1,0:T(8,128)(2,1)S(1)}, u32[]{:S(2)}, u32[]{:S(2)}) collective-permute-start(bf16[8,1024]{1,0:T(8,128)(2,1)S(1)} %collective-permute-done.7), channel_id=1, source_target_pairs={{0,1},{1,2},{2,3},{3,4},{4,5},{5,6},{6,7},{7,8},{8,9},{9,10},{10,1... | collective-permute-start | bytes 49160 | tf_op jit(solution)/shard_map/ppermute | solution.py:27
  143.8 5.9 %collective-permute-start.9 = (bf16[8,1024]{1,0:T(8,128)(2,1)S(1)}, bf16[8,1024]{1,0:T(8,128)(2,1)S(1)}, u32[]{:S(2)}, u32[]{:S(2)}) collective-permute-start(bf16[8,1024]{1,0:T(8,128)(2,1)S(1)} %collective-permute-done.8), channel_id=1, source_target_pairs={{0,1},{1,2},{2,3},{3,4},{4,5},{5,6},{6,7},{7,8},{8,9},{9,10},{10,1... | collective-permute-start | bytes 49160 | tf_op jit(solution)/shard_map/ppermute | solution.py:27
  149.7 5.9 %collective-permute-start.10 = (bf16[8,1024]{1,0:T(8,128)(2,1)S(1)}, bf16[8,1024]{1,0:T(8,128)(2,1)S(1)}, u32[]{:S(2)}, u32[]{:S(2)}) collective-permute-start(bf16[8,1024]{1,0:T(8,128)(2,1)S(1)} %collective-permute-done.9), channel_id=1, source_target_pairs={{0,1},{1,2},{2,3},{3,4},{4,5},{5,6},{6,7},{7,8},{8,9},{9,10},{10,1... | collective-permute-start | bytes 49160 | tf_op jit(solution)/shard_map/ppermute | solution.py:27
  155.6 5.9 %collective-permute-start.11 = (bf16[8,1024]{1,0:T(8,128)(2,1)S(1)}, bf16[8,1024]{1,0:T(8,128)(2,1)S(1)}, u32[]{:S(2)}, u32[]{:S(2)}) collective-permute-start(bf16[8,1024]{1,0:T(8,128)(2,1)S(1)} %collective-permute-done.10), channel_id=1, source_target_pairs={{0,1},{1,2},{2,3},{3,4},{4,5},{5,6},{6,7},{7,8},{8,9},{9,10},{10,1... | collective-permute-start | bytes 49160 | tf_op jit(solution)/shard_map/ppermute | solution.py:27
  161.5 5.9 %collective-permute-start.12 = (bf16[8,1024]{1,0:T(8,128)(2,1)S(1)}, bf16[8,1024]{1,0:T(8,128)(2,1)S(1)}, u32[]{:S(2)}, u32[]{:S(2)}) collective-permute-start(bf16[8,1024]{1,0:T(8,128)(2,1)S(1)} %collective-permute-done.11), channel_id=1, source_target_pairs={{0,1},{1,2},{2,3},{3,4},{4,5},{5,6},{6,7},{7,8},{8,9},{9,10},{10,1... | collective-permute-start | bytes 49160 | tf_op jit(solution)/shard_map/ppermute | solution.py:27
  167.4 5.9 %collective-permute-start.13 = (bf16[8,1024]{1,0:T(8,128)(2,1)S(1)}, bf16[8,1024]{1,0:T(8,128)(2,1)S(1)}, u32[]{:S(2)}, u32[]{:S(2)}) collective-permute-start(bf16[8,1024]{1,0:T(8,128)(2,1)S(1)} %collective-permute-done.12), channel_id=1, source_target_pairs={{0,1},{1,2},{2,3},{3,4},{4,5},{5,6},{6,7},{7,8},{8,9},{9,10},{10,1... | collective-permute-start | bytes 49160 | tf_op jit(solution)/shard_map/ppermute | solution.py:27
  173.3 14.2 %collective-permute-start.14 = (bf16[8,1024]{1,0:T(8,128)(2,1)S(1)}, bf16[8,1024]{1,0:T(8,128)(2,1)S(1)}, u32[]{:S(2)}, u32[]{:S(2)}) collective-permute-start(bf16[8,1024]{1,0:T(8,128)(2,1)S(1)} %collective-permute-done.13), channel_id=1, source_target_pairs={{0,1},{1,2},{2,3},{3,4},{4,5},{5,6},{6,7},{7,8},{8,9},{9,10},{10,1... | collective-permute-start | bytes 49160 | tf_op jit(solution)/shard_map/ppermute | solution.py:27
  176.2 6.3 %copy-start.2 = (s32[8,8]{1,0:T(8,128)S(1)}, s32[8,8]{1,0:T(8,128)}, u32[]{:S(2)}) copy-start(s32[8,8]{1,0:T(8,128)} %param.10) | copy-start | bytes 772
  176.2 24.8 %all-to-all-start.1 = ((bf16[8,128,1024]{1,0,2:T(8,128)(2,1)}), bf16[8,128,1024]{1,0,2:T(8,128)(2,1)S(1)}, u32[]{:S(2)}, u32[]{:S(2)}) async-start(bf16[8,128,1024]{1,0,2:T(8,128)(2,1)} %copy.22), calls=%async_computation.1 | async-start | bytes 4194304 | tf_op jit(solution)/shard_map/all_to_all | solution.py:21
  201.0 27.8 %all-to-all-start = ((bf16[8,128,1024]{1,0,2:T(8,128)(2,1)}), bf16[8,128,1024]{1,0,2:T(8,128)(2,1)}, u32[]{:S(2)}, u32[]{:S(2)}) async-start(bf16[8,128,1024]{1,0,2:T(8,128)(2,1)} %copy.20), calls=%async_computation | async-start | bytes 4194304 | tf_op jit(solution)/shard_map/all_to_all | solution.py:42
  207.7 187.4 %all-reduce.3.cloned.1.call-start = ((), (), s32[]{:S(2)}) async-start(), calls=%async_computation.4 | async-start | bytes 131072
Sparse Core Ops, SparseCore 0:
  10.3 68.8 all-gather.2
  90.0 87.6 all-gather.4
  243.2 151.8 all-reduce.2
